TPU v7x, 32 devices: a whole 2x2x4 slice. The times are simulated.
32 devices in a mesh: grp: 2 (over y), row: 4 (over z), col: 2 (over x), rep: 2 (over core).
Axes of the slice: x: 2, y: 2, z: 4, core: 2. Of those that a mesh axis runs over, the one named last changes fastest.
Arguments:
- shard_rows: bfloat16 [11520, 512], P(('grp', 'row', 'col', 'rep')), parts along dimension 0, may hold values from -24 to 24
- row_position: int32 [11520], P(('grp', 'row', 'col', 'rep')), parts along dimension 0, may hold values from 0 to 3071, as said below
- shard_count: int32 [32], P(('grp', 'row', 'col', 'rep')), parts along dimension 0, may hold values from 1 to 360, as said below
Outputs:
- max_similarity: float32 [6144], P(('grp', 'row', 'col', 'rep')), parts along dimension 0
There are 2 independent parts, one for each index of `grp`. A program takes and returns all parts, laid end to end along the dimension named above; each array names one. Nothing has to cross between parts.
Inputs may be any that keep to these rules, and one draw needn't show every extreme that they name: `row_position`: row j of shard s is used when j < shard_count[s]; the used rows of all shards hold every position 0 to 3071 once, unused rows hold arbitrary positions. At most 24 used rows of one shard have positions in one aligned run of 192 positions, and some shard reaches 24. `shard_count`: the counts sum to 3072.
All inputs are finite; a program needn't handle non-finite values.
Results may differ from a plain program's by a relative error of at most 0.00063.
Values may be sent and summed in bfloat16 or wider, within the bound.
A program may use at most 64 MiB of HBM per device.

v0:
```python
import math
import jax
import jax.numpy as jnp
from jax import lax
from jax.sharding import PartitionSpec as P

OWN = 192


def normalize(owned_rows):
    widened = owned_rows.astype(jnp.float32)
    return (widened / jnp.sqrt(jnp.sum(widened * widened, 1, keepdims=True) + 1e-06)).astype(
        jnp.bfloat16
    )


def body(shard_rows, row_position, shard_count):
    row_devices = lax.axis_size("row")
    cross_devices = lax.axis_size(("col", "rep"))
    all_shards = row_devices * cross_devices
    per_owner = OWN
    owner_load = max(1, per_owner // all_shards)
    slot_count = 2 * owner_load
    block_rows = per_owner * cross_devices
    capacity, feature = shard_rows.shape
    row_place = lax.axis_index("row")
    cross_place = lax.axis_index(("col", "rep"))
    is_used = jnp.arange(capacity) < shard_count[0]
    position = jnp.where(is_used, row_position, 0)
    owner_first = position // per_owner
    one_hot = jnp.logical_and(
        owner_first[:, None] == jnp.arange(all_shards)[None, :], is_used[:, None]
    ).astype(jnp.int32)
    ranking = jnp.sum(jnp.cumsum(one_hot, 0) * one_hot, 1) - 1
    target = jnp.where(is_used, owner_first * slot_count + ranking, all_shards * slot_count)
    packed = (
        jnp.zeros((all_shards * slot_count, feature), shard_rows.dtype)
        .at[target]
        .set(shard_rows, mode="drop")
    )
    placed = (
        jnp.full((all_shards * slot_count,), -1, jnp.int32).at[target].set(position, mode="drop")
    )
    first_packed = packed.reshape(row_devices, cross_devices, slot_count, feature)
    first_placed = placed.reshape(row_devices, cross_devices, slot_count)
    own_offset = row_place * block_rows + cross_place * per_owner
    received = (
        lax.all_to_all(
            lax.all_to_all(first_packed, "row", split_axis=0, concat_axis=0, tiled=True),
            ("col", "rep"),
            split_axis=1,
            concat_axis=1,
            tiled=True,
        ),
        lax.all_to_all(
            lax.all_to_all(first_placed, "row", split_axis=0, concat_axis=0, tiled=True),
            ("col", "rep"),
            split_axis=1,
            concat_axis=1,
            tiled=True,
        ),
    )
    flat_rows = received[0].reshape(-1, feature)
    flat_places = received[1].reshape(-1)
    local_index = jnp.where(flat_places >= 0, flat_places - own_offset, per_owner)
    owned_rows = (
        jnp.zeros((per_owner, feature), flat_rows.dtype).at[local_index].set(flat_rows, mode="drop")
    )
    row_owned = normalize(owned_rows)
    row_block = lax.all_gather(row_owned, ("col", "rep"), axis=0, tiled=True)
    column_index = jnp.arange(block_rows)
    column_block = lax.all_gather(row_owned, "row", axis=0, tiled=True)
    column_places = (
        column_index // per_owner * block_rows + cross_place * per_owner + column_index % per_owner
    )
    row_step = math.gcd(block_rows, 512)
    column_step = math.gcd(block_rows, 1024)

    def row_maxima(inputs):
        row_tile, row_start = inputs
        row_global = row_place * block_rows + row_start + jnp.arange(row_step)
        running = jnp.full((row_step,), -4.0, jnp.float32)
        for column_turn in range(block_rows // column_step):
            column_tile = column_block[column_turn * column_step : (column_turn + 1) * column_step]
            scores = jnp.einsum(
                "rd,cd->rc", row_tile, column_tile, preferred_element_type=jnp.float32
            )
            column_global = column_places[
                column_turn * column_step : (column_turn + 1) * column_step
            ]
            scores = jnp.where(row_global[:, None] == column_global[None, :], -4.0, scores)
            running = jnp.maximum(running, jnp.max(scores, 1))
        return running

    starts = jnp.arange(block_rows // row_step, dtype=jnp.int32) * row_step
    maxima = lax.map(row_maxima, (row_block.reshape(-1, row_step, feature), starts)).reshape(
        block_rows
    )
    combined = lax.pmax(maxima, ("col", "rep"))
    return lax.dynamic_slice_in_dim(combined, cross_place * per_owner, per_owner)


def solution(mesh):
    return jax.shard_map(
        body,
        mesh=mesh,
        in_specs=(
            P(("grp", "row", "col", "rep"), None),
            P(("grp", "row", "col", "rep")),
            P(("grp", "row", "col", "rep")),
        ),
        out_specs=P(("grp", "row", "col", "rep")),
        check_vma=False,
    )
```

profile of v0, /device:TPU:0, one launch (start us, length us, event | category | flops | bytes accessed | tf_op | source)
XLA Modules:
  0.0 92.6 jit_solution(1535740901777857113)
XLA Ops:
  0.7 0.7 copy-done
  1.4 0.9 reduce-window.6
  2.6 2.9 %scatter_custom_fusion = s32[384]{0:T(512)S(1)} fusion(s32[360]{0:T(512)S(1)} %compare_select_fusion.1, s32[360]{0:T(512)S(1)} %get-tuple-element.104, s32[]{:T(128)} %constant.84.clone.1), kind=kCustom, calls=%fused_computation.67 | custom fusion | bytes 1540 | tf_op jit(solution)/shard_map/scatter | solution.py:42
  5.5 0.7 reshape.115
  6.2 6.3 %all-to-all-start = ((s32[4,4,24]{2,1,0:T(4,128)}), s32[4,4,24]{2,1,0:T(4,128)S(1)}, u32[]{:S(2)}, u32[]{:S(2)}) async-start(s32[4,4,24]{2,1,0:T(4,128)} %reshape.115), calls=%async_computation | async-start | bytes 16384 | tf_op jit(solution)/shard_map/all_to_all | solution.py:56
  12.6 3.0 %scatter_custom_fusion.1 = bf16[384,512]{1,0:T(8,128)(2,1)} fusion(s32[360]{0:T(512)S(1)} %compare_select_fusion.1, bf16[360,512]{1,0:T(8,128)(2,1)} %param.5, bf16[]{:T(256)} %constant.83.clone.1), kind=kCustom, calls=%fused_computation.27 | custom fusion | bytes 393728 | tf_op jit(solution)/shard_map/scatter | solution.py:39
  15.6 2.6 %all-to-all-done = s32[4,4,24]{2,1,0:T(4,128)S(1)} async-done(((s32[4,4,24]{2,1,0:T(4,128)}), s32[4,4,24]{2,1,0:T(4,128)S(1)}, u32[]{:S(2)}, u32[]{:S(2)}) %all-to-all-start) | async-done | bytes 1568 | tf_op jit(solution)/shard_map/all_to_all | solution.py:56
  18.2 3.5 %all-to-all-start.2 = ((bf16[4,4,24,512]{3,2,1,0:T(8,128)(2,1)}), bf16[4,4,24,512]{3,2,1,0:T(8,128)(2,1)S(1)}, u32[]{:S(2)}, u32[]{:S(2)}) async-start(bf16[4,4,24,512]{3,2,1,0:T(8,128)(2,1)} %bitcast.5), calls=%async_computation.2 | async-start | bytes 786432 | tf_op jit(solution)/shard_map/all_to_all | solution.py:49
  21.6 0.6 copy.17
  22.2 9.9 %all-to-all-done.2 = bf16[4,4,24,512]{3,2,1,0:T(8,128)(2,1)S(1)} async-done(((bf16[4,4,24,512]{3,2,1,0:T(8,128)(2,1)}), bf16[4,4,24,512]{3,2,1,0:T(8,128)(2,1)S(1)}, u32[]{:S(2)}, u32[]{:S(2)}) %all-to-all-start.2) | async-done | bytes 393248 | tf_op jit(solution)/shard_map/all_to_all | solution.py:49
  32.1 3.2 %all-to-all-start.1 = ((s32[4,4,24]{2,0,1:T(4,128)}), s32[4,4,24]{2,0,1:T(4,128)S(1)}, u32[]{:S(2)}, u32[]{:S(2)}) async-start(s32[4,4,24]{2,0,1:T(4,128)} %copy.17), calls=%async_computation.1 | async-start | bytes 16384 | tf_op jit(solution)/shard_map/all_to_all | solution.py:55
  35.4 0.8 copy.19
  36.2 3.0 %all-to-all-done.1 = s32[4,4,24]{2,0,1:T(4,128)S(1)} async-done(((s32[4,4,24]{2,0,1:T(4,128)}), s32[4,4,24]{2,0,1:T(4,128)S(1)}, u32[]{:S(2)}, u32[]{:S(2)}) %all-to-all-start.1) | async-done | bytes 1568 | tf_op jit(solution)/shard_map/all_to_all | solution.py:55
  39.1 3.5 %all-to-all-start.3 = ((bf16[4,4,24,512]{3,2,0,1:T(8,128)(2,1)}), bf16[4,4,24,512]{3,2,0,1:T(8,128)(2,1)S(1)}, u32[]{:S(2)}, u32[]{:S(2)}) async-start(bf16[4,4,24,512]{3,2,0,1:T(8,128)(2,1)} %copy.19), calls=%async_computation.3 | async-start | bytes 786432 | tf_op jit(solution)/shard_map/all_to_all | solution.py:48
  42.7 7.3 %all-to-all-done.3 = bf16[4,4,24,512]{3,2,0,1:T(8,128)(2,1)S(1)} async-done(((bf16[4,4,24,512]{3,2,0,1:T(8,128)(2,1)}), bf16[4,4,24,512]{3,2,0,1:T(8,128)(2,1)S(1)}, u32[]{:S(2)}, u32[]{:S(2)}) %all-to-all-start.3) | async-done | bytes 393248 | tf_op jit(solution)/shard_map/all_to_all | solution.py:48
  50.0 2.0 %scatter_custom_fusion.2 = bf16[192,512]{1,0:T(8,128)(2,1)S(1)} fusion(s32[384]{0:T(512)S(1)} %fusion.35, bf16[384,512]{1,0:T(8,128)(2,1)S(1)} %bitcast.40, bf16[]{:T(256)} %constant.83.clone.1), kind=kCustom, calls=%fused_computation.29 | custom fusion | bytes 196610 | tf_op jit(solution)/shard_map/scatter | solution.py:67
  52.3 18.0 %all_gather.7 = bf16[768,512]{1,0:T(8,128)(2,1)S(1)} all-gather(bf16[192,512]{1,0:T(8,128)(2,1)S(1)} %fusion.16), channel_id=1, replica_groups=mesh['grp'=2,'row'=4,'col'=2,'rep'=2] {'row'}, dimensions={0}, use_global_device_ids=true | all-gather | bytes 983040 | tf_op jit(solution)/shard_map/all_gather | solution.py:72
  70.3 7.5 %all_gather.6 = bf16[768,512]{1,0:T(8,128)(2,1)S(1)} all-gather(bf16[192,512]{1,0:T(8,128)(2,1)S(1)} %fusion.16), channel_id=1, replica_groups=mesh['grp'=2,'row'=4,'col'=2,'rep'=2] {'col','rep'}, dimensions={0}, use_global_device_ids=true | all-gather | bytes 983040 | tf_op jit(solution)/shard_map/all_gather | solution.py:70
  77.8 6.9 %while.12 = (s32[]{:T(128)}, f32[3,256]{1,0:T(4,128)S(1)}, s32[3]{0:T(128)S(1)}, s32[]{:T(128)}, s32[768]{0:T(1024)S(1)}, /*index=5*/bf16[3,256,512]{2,1,0:T(8,1...) while((s32[]{:T(128)}, f32[3,256]{1,0:T(4,128)S(1)}, s32[3]{0:T(128)S(1)}, s32[]{:T(128)}, ...), condition=%wide.region_11.12_spmd, body=%wide.region_7.11_spmd.sunk | while | flops 201916672 | bytes 1595529 | solution.py:96
  77.8 0.7 dynamic_slice.35
  80.1 0.7 dynamic_slice.35
  82.3 0.7 dynamic_slice.35
  84.6 7.3 %pmax.7 = f32[768]{0:T(1024)S(1)} all-reduce(f32[768]{0:T(1024)S(1)} %reshape.119), channel_id=1, replica_groups=mesh['grp'=2,'row'=4,'col'=2,'rep'=2] {'col','rep'}, use_global_device_ids=true, to_apply=%region_12.13 | all-reduce | flops 768 | bytes 6144 | tf_op jit(solution)/shard_map/pmax | solution.py:99
  91.9 0.6 dynamic_slice.15
  (40 shorter events, 3.5 us)
Async XLA Ops:
  0.7 0.7 copy-start
  6.2 11.9 %all-to-all-start = ((s32[4,4,24]{2,1,0:T(4,128)}), s32[4,4,24]{2,1,0:T(4,128)S(1)}, u32[]{:S(2)}, u32[]{:S(2)}) async-start(s32[4,4,24]{2,1,0:T(4,128)} %reshape.115), calls=%async_computation | async-start | bytes 16384 | tf_op jit(solution)/shard_map/all_to_all | solution.py:56
  18.2 14.0 %all-to-all-start.2 = ((bf16[4,4,24,512]{3,2,1,0:T(8,128)(2,1)}), bf16[4,4,24,512]{3,2,1,0:T(8,128)(2,1)S(1)}, u32[]{:S(2)}, u32[]{:S(2)}) async-start(bf16[4,4,24,512]{3,2,1,0:T(8,128)(2,1)} %bitcast.5), calls=%async_computation.2 | async-start | bytes 786432 | tf_op jit(solution)/shard_map/all_to_all | solution.py:49
  32.1 7.0 %all-to-all-start.1 = ((s32[4,4,24]{2,0,1:T(4,128)}), s32[4,4,24]{2,0,1:T(4,128)S(1)}, u32[]{:S(2)}, u32[]{:S(2)}) async-start(s32[4,4,24]{2,0,1:T(4,128)} %copy.17), calls=%async_computation.1 | async-start | bytes 16384 | tf_op jit(solution)/shard_map/all_to_all | solution.py:55
  39.1 10.9 %all-to-all-start.3 = ((bf16[4,4,24,512]{3,2,0,1:T(8,128)(2,1)}), bf16[4,4,24,512]{3,2,0,1:T(8,128)(2,1)S(1)}, u32[]{:S(2)}, u32[]{:S(2)}) async-start(bf16[4,4,24,512]{3,2,0,1:T(8,128)(2,1)} %copy.19), calls=%async_computation.3 | async-start | bytes 786432 | tf_op jit(solution)/shard_map/all_to_all | solution.py:48
where the time goes:
time: 93.1 us; the launch traced here: 92.6 us
  blocking collectives  32.8 us (35%)
  waiting for transfers between devices  22.7 us (24%)
  starting transfers between devices  16.5 us (18%)
  local copies, waits for them, and re-layouts  13.7 us (15%)
  matrix products  2.53 us (3%)
  loops' own time  2.18 us (2%)
  other arithmetic  1.38 us (1%)
    all_gather x1, blocking collectives, body(): column_block = lax.all_gather(row_owned, 'row', axis=0, tiled=True)  18 us
    all_to_all x1, waiting for transfers between devices, body(): lax.all_to_all(first_packed, 'row', split_axis=0, concat_axis=0, tiled=True)  9.87 us
    all_gather x1, blocking collectives, body(): row_block = lax.all_gather(row_owned, ('col', 'rep'), axis=0, tiled=True)  7.46 us
    pmax x1, blocking collectives, body(): combined = lax.pmax(maxima, ('col', 'rep'))  7.28 us
    all_to_all x1, waiting for transfers between devices, body(): lax.all_to_all(lax.all_to_all(first_packed, 'row', split_axis=0, concat_a...  7.27 us
    all_to_all x1, starting transfers between devices, body(): lax.all_to_all(first_placed, 'row', split_axis=0, concat_axis=0, tiled=True)  6.32 us
    all_to_all x1, starting transfers between devices, body(): lax.all_to_all(lax.all_to_all(first_packed, 'row', split_axis=0, concat_a...  3.46 us
    all_to_all x1, starting transfers between devices, body(): lax.all_to_all(first_packed, 'row', split_axis=0, concat_axis=0, tiled=True)  3.46 us
  transfers between devices with their start and end apart: 4, of which 4 were waited for; matrix products, arithmetic and copies ran while one was open for 5% of the time, Pallas kernels for 0%

commit v1 on v0

--- a/solution.py
+++ b/solution.py
@@ -5,6 +5,22 @@
 from jax.sharding import PartitionSpec as P
 
 OWN = 192
+
+
+def swapped_with_each(array, axis, split, join):
+    ways, here = (lax.axis_size(axis), lax.axis_index(axis))
+    width = array.shape[split] // ways
+    shape = list(array.shape)
+    shape[split] = width
+    height = shape[join]
+    shape[join] = height * ways
+    full = jnp.zeros(shape, array.dtype)
+    for mask in range(ways):
+        part = lax.dynamic_slice_in_dim(array, (here ^ mask) * width, width, axis=split)
+        if mask:
+            part = lax.ppermute(part, axis, [(d, d ^ mask) for d in range(ways)])
+        full = lax.dynamic_update_slice_in_dim(full, part, (here ^ mask) * height, axis=join)
+    return full
 
 
 def normalize(owned_rows):
@@ -46,7 +62,7 @@
     own_offset = row_place * block_rows + cross_place * per_owner
     received = (
         lax.all_to_all(
-            lax.all_to_all(first_packed, "row", split_axis=0, concat_axis=0, tiled=True),
+            swapped_with_each(first_packed, "row", 0, 0),
             ("col", "rep"),
             split_axis=1,
             concat_axis=1,

time: 93.1 us -> 86 us (0.924)
  waiting for transfers between devices: 22.7 us -> 13.2 us
  local copies, waits for them, and re-layouts: 13.7 us -> 15.7 us
  starting transfers between devices: 16.5 us -> 17.5 us
    all_to_all x2 -> x1, waiting for transfers between devices: 17.1 us -> 7.27 us  [body(): lax.all_to_all(swapped_with_each(first_packed, 'row', 0, 0), ('col', 'rep...]
    ppermute x0 -> x3, starting transfers between devices: none -> 5.68 us  [swapped_with_each(): part = lax.ppermute(part, axis, [(d, d ^ mask) for d in range(ways)])]
    all_to_all x2 -> x1, starting transfers between devices: 6.92 us -> 3.46 us  [body(): lax.all_to_all(swapped_with_each(first_packed, 'row', 0, 0), ('col', 'rep...]
    dynamic_update_slice x0 -> x4, local copies, waits for them, and re-layouts: none -> 2.61 us  [swapped_with_each(): lax.dynamic_update_slice_in_dim(full, part, (here ^ mask) * height, axis=...]
    all_to_all x1, waiting for transfers between devices: 2.57 us -> 4.14 us  [body(): lax.all_to_all(first_placed, 'row', split_axis=0, concat_axis=0, tiled=True)]
    all_to_all x1, starting transfers between devices: 6.32 us -> 5.09 us  [body(): lax.all_to_all(first_placed, 'row', split_axis=0, concat_axis=0, tiled=True)]
    all_to_all x1, waiting for transfers between devices: 2.98 us -> 1.81 us  [body(): lax.all_to_all(lax.all_to_all(first_placed, 'row', split_axis=0, concat_a...]
  transfers between devices with their start and end apart: 4 -> 6, of which waited for: 4 -> 3; matrix products, arithmetic and copies ran while one was open for 5% -> 9% of each run, Pallas kernels for 0% -> 0%
where the time goes in v1:
time: 86 us; the launch traced here: 85.6 us
  blocking collectives  32.3 us (38%)
  starting transfers between devices  17.5 us (20%)
  local copies, waits for them, and re-layouts  15.7 us (18%)
  waiting for transfers between devices  13.2 us (15%)
  matrix products  2.52 us (3%)
  loops' own time  2.18 us (3%)
  other arithmetic  1.38 us (2%)
    all_gather x1, blocking collectives, body(): column_block = lax.all_gather(row_owned, 'row', axis=0, tiled=True)  17.5 us
    all_gather x1, blocking collectives, body(): row_block = lax.all_gather(row_owned, ('col', 'rep'), axis=0, tiled=True)  7.67 us
    all_to_all x1, waiting for transfers between devices, body(): lax.all_to_all(swapped_with_each(first_packed, 'row', 0, 0), ('col', 'rep...  7.27 us
    pmax x1, blocking collectives, body(): combined = lax.pmax(maxima, ('col', 'rep'))  7.06 us
    ppermute x3, starting transfers between devices, swapped_with_each(): part = lax.ppermute(part, axis, [(d, d ^ mask) for d in range(ways)])  5.68 us
    all_to_all x1, starting transfers between devices, body(): lax.all_to_all(first_placed, 'row', split_axis=0, concat_axis=0, tiled=True)  5.09 us
    all_to_all x1, waiting for transfers between devices, body(): lax.all_to_all(first_placed, 'row', split_axis=0, concat_axis=0, tiled=True)  4.14 us
    all_to_all x1, starting transfers between devices, body(): lax.all_to_all(swapped_with_each(first_packed, 'row', 0, 0), ('col', 'rep...  3.46 us
  transfers between devices with their start and end apart: 6, of which 3 were waited for; matrix products, arithmetic and copies ran while one was open for 9% of the time, Pallas kernels for 0%

profile of v1, /device:TPU:0, one launch (start us, length us, event | category | flops | bytes accessed | tf_op | source)
XLA Modules:
  0.0 85.6 jit_solution(15909123457426097906)
XLA Ops:
  0.7 0.7 copy-done
  1.4 0.9 %reduce-window.6 = s32[16,3,128]{2,0,1:T(8,128)S(1)} reduce-window(s32[16,3,128]{2,0,1:T(8,128)S(1)} %copy_bitcast_fusion, s32[]{:T(128)} %constant.85.clone.1), window={size=1x1x128 pad=0_0x0_0x127_0}, to_apply=%region_0.1 | reduce-window | flops 780288 | bytes 49156 | tf_op jit(solution)/shard_map/reduce-window
  2.6 2.4 %scatter_custom_fusion.1 = bf16[384,512]{1,0:T(8,128)(2,1)S(1)} fusion(s32[360]{0:T(512)S(1)} %compare_select_fusion.1, bf16[360,512]{1,0:T(8,128)(2,1)} %param.5, bf16[]{:T(256)} %constant.87.clone.1), kind=kCustom, calls=%fused_computation.27 | custom fusion | bytes 393728 | tf_op jit(solution)/shard_map/scatter | solution.py:55
  5.1 3.1 %collective-permute-start = (bf16[1,4,24,512]{3,2,0,1:T(8,128)(2,1)S(1)}, bf16[1,4,24,512]{3,2,0,1:T(8,128)(2,1)S(1)}, u32[]{:S(2)}, u32[]{:S(2)}) collective-permute-start(bf16[1,4,24,512]{3,2,0,1:T(8,128)(2,1)S(1)} %get-tuple-element.111), channel_id=1, source_target_pairs={{0,4},{4,0},{8,12},{12,8},{1,5},{5,1},{9,13},{13,9},{2,6},{6,2},{1... | collective-permute-start | bytes 294920 | tf_op jit(solution)/shard_map/ppermute | solution.py:21
  8.2 2.6 %collective-permute-start.1 = (bf16[1,4,24,512]{3,2,0,1:T(8,128)(2,1)S(1)}, bf16[1,4,24,512]{3,2,0,1:T(8,128)(2,1)S(1)}, u32[]{:S(2)}, u32[]{:S(2)}) collective-permute-start(bf16[1,4,24,512]{3,2,0,1:T(8,128)(2,1)S(1)} %get-tuple-element.110), channel_id=1, source_target_pairs={{0,8},{4,12},{8,0},{12,4},{1,9},{5,13},{9,1},{13,5},{2,10},{6,14},... | collective-permute-start | bytes 294920 | tf_op jit(solution)/shard_map/ppermute | solution.py:21
  10.8 2.9 %scatter_custom_fusion = s32[384]{0:T(512)S(1)} fusion(s32[360]{0:T(512)S(1)} %compare_select_fusion.1, s32[360]{0:T(512)S(1)} %get-tuple-element.104, s32[]{:T(128)} %constant.88.clone.1), kind=kCustom, calls=%fused_computation.74 | custom fusion | bytes 1540 | tf_op jit(solution)/shard_map/scatter | solution.py:58
  13.7 0.7 reshape.115
  14.4 5.1 %all-to-all-start = ((s32[4,4,24]{2,1,0:T(4,128)}), s32[4,4,24]{2,1,0:T(4,128)S(1)}, u32[]{:S(2)}, u32[]{:S(2)}) async-start(s32[4,4,24]{2,1,0:T(4,128)} %reshape.115), calls=%async_computation | async-start | bytes 16384 | tf_op jit(solution)/shard_map/all_to_all | solution.py:72
  19.5 0.8 broadcast_in_dim.74
  20.3 0.7 bitcast_dynamic-update-slice_fusion
  20.9 4.1 %all-to-all-done = s32[4,4,24]{2,1,0:T(4,128)S(1)} async-done(((s32[4,4,24]{2,1,0:T(4,128)}), s32[4,4,24]{2,1,0:T(4,128)S(1)}, u32[]{:S(2)}, u32[]{:S(2)}) %all-to-all-start) | async-done | bytes 1568 | tf_op jit(solution)/shard_map/all_to_all | solution.py:72
  25.7 3.2 %all-to-all-start.1 = ((s32[4,4,24]{2,0,1:T(4,128)}), s32[4,4,24]{2,0,1:T(4,128)S(1)}, u32[]{:S(2)}, u32[]{:S(2)}) async-start(s32[4,4,24]{2,0,1:T(4,128)} %copy.14), calls=%async_computation.1 | async-start | bytes 16384 | tf_op jit(solution)/shard_map/all_to_all | solution.py:71
  28.9 0.7 constant_dynamic-update-slice_fusion.2
  30.9 1.8 %all-to-all-done.1 = s32[4,4,24]{2,0,1:T(4,128)S(1)} async-done(((s32[4,4,24]{2,0,1:T(4,128)}), s32[4,4,24]{2,0,1:T(4,128)S(1)}, u32[]{:S(2)}, u32[]{:S(2)}) %all-to-all-start.1) | async-done | bytes 1568 | tf_op jit(solution)/shard_map/all_to_all | solution.py:71
  32.7 3.5 %all-to-all-start.2 = ((bf16[4,4,24,512]{3,2,0,1:T(8,128)(2,1)}), bf16[4,4,24,512]{3,2,0,1:T(8,128)(2,1)S(1)}, u32[]{:S(2)}, u32[]{:S(2)}) async-start(bf16[4,4,24,512]{3,2,0,1:T(8,128)(2,1)} %constant_dynamic-update-slice_fusion), calls=%async_computation.2 | async-start | bytes 786432 | tf_op jit(solution)/shard_map/all_to_all | solution.py:64
  36.3 7.3 %all-to-all-done.2 = bf16[4,4,24,512]{3,2,0,1:T(8,128)(2,1)S(1)} async-done(((bf16[4,4,24,512]{3,2,0,1:T(8,128)(2,1)}), bf16[4,4,24,512]{3,2,0,1:T(8,128)(2,1)S(1)}, u32[]{:S(2)}, u32[]{:S(2)}) %all-to-all-start.2) | async-done | bytes 393248 | tf_op jit(solution)/shard_map/all_to_all | solution.py:64
  43.6 2.0 %scatter_custom_fusion.2 = bf16[192,512]{1,0:T(8,128)(2,1)S(1)} fusion(s32[384]{0:T(512)S(1)} %fusion.35, bf16[384,512]{1,0:T(8,128)(2,1)S(1)} %bitcast.50, bf16[]{:T(256)} %constant.87.clone.1), kind=kCustom, calls=%fused_computation.33 | custom fusion | bytes 196610 | tf_op jit(solution)/shard_map/scatter | solution.py:83
  45.8 17.5 %all_gather.7 = bf16[768,512]{1,0:T(8,128)(2,1)S(1)} all-gather(bf16[192,512]{1,0:T(8,128)(2,1)S(1)} %fusion.16), channel_id=1, replica_groups=mesh['grp'=2,'row'=4,'col'=2,'rep'=2] {'row'}, dimensions={0}, use_global_device_ids=true | all-gather | bytes 983040 | tf_op jit(solution)/shard_map/all_gather | solution.py:88
  63.4 7.7 %all_gather.6 = bf16[768,512]{1,0:T(8,128)(2,1)S(1)} all-gather(bf16[192,512]{1,0:T(8,128)(2,1)S(1)} %fusion.16), channel_id=1, replica_groups=mesh['grp'=2,'row'=4,'col'=2,'rep'=2] {'col','rep'}, dimensions={0}, use_global_device_ids=true | all-gather | bytes 983040 | tf_op jit(solution)/shard_map/all_gather | solution.py:86
  71.0 6.9 %while.12 = (s32[]{:T(128)}, f32[3,256]{1,0:T(4,128)S(1)}, s32[3]{0:T(128)S(1)}, s32[]{:T(128)}, s32[768]{0:T(1024)S(1)}, /*index=5*/bf16[3,256,512]{2,1,0:T(8,1...) while((s32[]{:T(128)}, f32[3,256]{1,0:T(4,128)S(1)}, s32[3]{0:T(128)S(1)}, s32[]{:T(128)}, ...), condition=%wide.region_11.12_spmd, body=%wide.region_7.11_spmd.sunk | while | flops 201916672 | bytes 1595529 | solution.py:112
  71.0 0.7 dynamic_slice.55
  73.3 0.7 dynamic_slice.55
  75.6 0.7 dynamic_slice.55
  77.9 7.1 %pmax.7 = f32[768]{0:T(1024)S(1)} all-reduce(f32[768]{0:T(1024)S(1)} %reshape.119), channel_id=1, replica_groups=mesh['grp'=2,'row'=4,'col'=2,'rep'=2] {'col','rep'}, use_global_device_ids=true, to_apply=%region_12.13 | all-reduce | flops 768 | bytes 6144 | tf_op jit(solution)/shard_map/pmax | solution.py:115
  (49 shorter events, 6.1 us)
Async XLA Ops:
  0.7 0.7 copy-start
  5.1 23.8 %collective-permute-start = (bf16[1,4,24,512]{3,2,0,1:T(8,128)(2,1)S(1)}, bf16[1,4,24,512]{3,2,0,1:T(8,128)(2,1)S(1)}, u32[]{:S(2)}, u32[]{:S(2)}) collective-permute-start(bf16[1,4,24,512]{3,2,0,1:T(8,128)(2,1)S(1)} %get-tuple-element.111), channel_id=1, source_target_pairs={{0,4},{4,0},{8,12},{12,8},{1,5},{5,1},{9,13},{13,9},{2,6},{6,2},{1... | collective-permute-start | bytes 294920 | tf_op jit(solution)/shard_map/ppermute | solution.py:21
  8.2 21.4 %collective-permute-start.1 = (bf16[1,4,24,512]{3,2,0,1:T(8,128)(2,1)S(1)}, bf16[1,4,24,512]{3,2,0,1:T(8,128)(2,1)S(1)}, u32[]{:S(2)}, u32[]{:S(2)}) collective-permute-start(bf16[1,4,24,512]{3,2,0,1:T(8,128)(2,1)S(1)} %get-tuple-element.110), channel_id=1, source_target_pairs={{0,8},{4,12},{8,0},{12,4},{1,9},{5,13},{9,1},{13,5},{2,10},{6,14},... | collective-permute-start | bytes 294920 | tf_op jit(solution)/shard_map/ppermute | solution.py:21
  10.8 19.5 %collective-permute-start.2 = (bf16[1,4,24,512]{3,2,0,1:T(8,128)(2,1)S(1)}, bf16[1,4,24,512]{3,2,0,1:T(8,128)(2,1)S(1)}, u32[]{:S(2)}, u32[]{:S(2)}) collective-permute-start(bf16[1,4,24,512]{3,2,0,1:T(8,128)(2,1)S(1)} %get-tuple-element.109), channel_id=1, source_target_pairs={{0,12},{4,8},{8,4},{12,0},{1,13},{5,9},{9,5},{13,1},{2,14},{6,10},... | collective-permute-start | bytes 294920 | tf_op jit(solution)/shard_map/ppermute | solution.py:21
  14.4 10.7 %all-to-all-start = ((s32[4,4,24]{2,1,0:T(4,128)}), s32[4,4,24]{2,1,0:T(4,128)S(1)}, u32[]{:S(2)}, u32[]{:S(2)}) async-start(s32[4,4,24]{2,1,0:T(4,128)} %reshape.115), calls=%async_computation | async-start | bytes 16384 | tf_op jit(solution)/shard_map/all_to_all | solution.py:72
  25.7 7.0 %all-to-all-start.1 = ((s32[4,4,24]{2,0,1:T(4,128)}), s32[4,4,24]{2,0,1:T(4,128)S(1)}, u32[]{:S(2)}, u32[]{:S(2)}) async-start(s32[4,4,24]{2,0,1:T(4,128)} %copy.14), calls=%async_computation.1 | async-start | bytes 16384 | tf_op jit(solution)/shard_map/all_to_all | solution.py:71
  32.7 10.9 %all-to-all-start.2 = ((bf16[4,4,24,512]{3,2,0,1:T(8,128)(2,1)}), bf16[4,4,24,512]{3,2,0,1:T(8,128)(2,1)S(1)}, u32[]{:S(2)}, u32[]{:S(2)}) async-start(bf16[4,4,24,512]{3,2,0,1:T(8,128)(2,1)} %constant_dynamic-update-slice_fusion), calls=%async_computation.2 | async-start | bytes 786432 | tf_op jit(solution)/shard_map/all_to_all | solution.py:64
